TPU v7x, 32 devices: a whole 2x2x4 slice. The times are simulated.
32 devices in a mesh: occ: 16 (over z, y, core), vir: 2 (over x).
Axes of the slice: x: 2, y: 2, z: 4, core: 2. Of those that a mesh axis runs over, the one named last changes fastest.
Arguments:
- lambda_triples: bfloat16 [256, 320, 320], P('occ', 'vir'), may hold values from -6 to 6
- amplitude_triples: bfloat16 [256, 320, 320], P('occ', 'vir'), may hold values from -6 to 6
- spin_extent: int32 [256], P('occ'), may hold values from 80 to 320
- ladder_weight: bfloat16 [320, 320], P(None, 'vir'), may hold values from -0.3125 to 0.3125
- cycle_weight: bfloat16 [320, 40], replicated, may hold values from -0.3125 to 0.3125
- lambda_doubles: bfloat16 [40, 320], P(None, 'vir'), may hold values from -1 to 1
Outputs:
- residual: bfloat16 [256, 320, 320], P('occ', 'vir')
All inputs are finite; a program needn't handle non-finite values.
Results may differ from a plain program's by a relative error of at most 0.0043.
Values may be sent and summed in bfloat16 or wider, within the bound.
No kernel may reach another device: no remote copies, remote signals or barrier semaphores. Data moves between devices by JAX's collectives and lax.ppermute only.
A program may use at most 64 MiB of HBM per device.

v0:
```python
import jax
import jax.numpy as jnp
from jax import lax
from jax.sharding import PartitionSpec as P


def on_device(
    lambda_triples, amplitude_triples, spin_extent, ladder_weight, cycle_weight, lambda_doubles
):
    f32 = jnp.float32
    width = lambda_triples.shape[2]
    triples_all = lambda_triples.shape[0] * lax.axis_size("occ")
    columns = jnp.arange(width, dtype=jnp.int32)
    keep = columns[None, :] < spin_extent[:, None]
    masked = jnp.where(keep[:, None, :], lambda_triples, jnp.zeros_like(lambda_triples))
    ladder_full, doubles_full = (
        lax.all_gather(ladder_weight, "vir", axis=1, tiled=True),
        lax.all_gather(lambda_doubles, "vir", axis=1, tiled=True),
    )
    ladder_term = jnp.einsum("tae,eb->tab", masked, ladder_full, preferred_element_type=f32)
    cycle_mid = jnp.einsum(
        "tae,em->tam", amplitude_triples, cycle_weight, preferred_element_type=f32
    ).astype(jnp.bfloat16)
    cycle_term = jnp.einsum("tam,mb->tab", cycle_mid, doubles_full, preferred_element_type=f32)
    partial_density = jnp.einsum(
        "tae,tbe->ab",
        masked,
        lax.all_gather(amplitude_triples, "vir", axis=1, tiled=True),
        preferred_element_type=f32,
    )
    density = lax.psum(partial_density, "occ")
    density = (density / jnp.sqrt(f32(triples_all * width))).astype(jnp.bfloat16)
    density_term = jnp.einsum(
        "ac,tcb->tab",
        density,
        lax.all_gather(masked, "vir", axis=1, tiled=True),
        preferred_element_type=f32,
    )
    density_term = density_term / jnp.sqrt(f32(width))
    return (ladder_term + cycle_term + density_term).astype(jnp.bfloat16)


def solution(mesh):
    return jax.shard_map(
        on_device,
        mesh=mesh,
        in_specs=(
            P("occ", "vir", None),
            P("occ", "vir", None),
            P("occ"),
            P(None, "vir"),
            P(),
            P(None, "vir"),
        ),
        out_specs=P("occ", "vir", None),
        check_vma=False,
    )
```

profile of v0, /device:TPU:8, one launch (start us, length us, event | category | flops | bytes accessed | tf_op | source)
XLA Modules:
  0.0 227.4 jit_solution(11360172198900712387)
XLA Ops:
  6.5 0.0 copy-start
  6.5 0.0 copy-start.3
  6.5 0.0 copy-start.2
  6.5 0.0 all-gather.6.cloned.1.call-start
  6.5 0.7 all-gather.6.cloned.1.call-update
  7.3 0.0 all-gather.4.cloned.1.call-start
  7.3 0.7 iota_compare_fusion
  8.0 3.0 %broadcast_select_fusion = bf16[16,160,320]{2,1,0:T(8,128)(2,1)} fusion(bf16[16,160,320]{2,1,0:T(8,128)(2,1)} %param.6, pred[16,320]{1,0:T(8,128)(4,1)S(1)} %iota_compare_fusion), kind=kLoop, calls=%fused_computation.2 | loop fusion | flops 819200 | bytes 3281920 | tf_op jit(solution)/shard_map/jit(_where)/select_n | solution.py:15
  11.1 0.0 copy-start.1
  11.1 0.0 all-gather.4.cloned.1.call-update
  11.1 0.0 all-reduce.2.cloned.1.call-start
  11.2 0.0 copy-done.3
  11.2 4.6 %all-gather = bf16[2,160,40]{1,2,0:T(8,128)(2,1)S(1)} all-gather(bf16[1,160,40]{1,2,0:T(8,128)(2,1)S(1)} %bitcast.27), channel_id=1, replica_groups=mesh['occ'=16,'vir'=2] {'vir'}, dimensions={0}, use_global_device_ids=true | all-gather | bytes 38400 | tf_op jit(solution)/shard_map/all_gather | solution.py:18
  15.8 0.1 reshape.21
  15.9 0.0 copy-done.2
  15.9 6.4 %all_gather.12 = bf16[320,320]{0,1:T(8,128)(2,1)S(1)} all-gather(bf16[320,160]{0,1:T(8,128)(2,1)S(1)} %copy-done.2), channel_id=1, replica_groups=mesh['occ'=16,'vir'=2] {'vir'}, dimensions={1}, use_global_device_ids=true | all-gather | bytes 307200 | tf_op jit(solution)/shard_map/all_gather | solution.py:17
  22.3 4.9 %fusion.2 = f32[16,160,320]{2,1,0:T(8,128)} fusion(bf16[16,160,320]{2,1,0:T(8,128)(2,1)} %broadcast_select_fusion, bf16[320,320]{0,1:T(8,128)(2,1)S(1)} %all_gather.12), kind=kOutput, calls=%fused_computation.6 | convolution fusion | flops 524288000 | bytes 5120000 | tf_op jit(solution)/shard_map/tae,eb->tab/dot_general | solution.py:20
  27.2 36.7 %all-gather.6.cloned.1.call-done = bf16[16,320,320]{2,1,0:T(8,128)(2,1)} async-done(((bf16[16,160,320]{2,1,0:T(8,128)(2,1)}), bf16[16,320,320]{2,1,0:T(8,128)(2,1)}) %all-gather.6.cloned.1.call-update) | async-done | bytes 3276816 | tf_op jit(solution)/shard_map/all_gather | solution.py:28
  63.9 0.0 copy-done.1
  63.9 4.4 %convolution_bitcast_fusion = f32[160,320]{1,0:T(8,128)} fusion(bf16[16,160,320]{2,1,0:T(8,128)(2,1)S(1)} %copy-done.1, bf16[16,320,320]{2,1,0:T(8,128)(2,1)} %all-gather.6.cloned.1.call-done), kind=kOutput, calls=%fused_computation.5 | convolution fusion | flops 524288000 | bytes 5120000 | tf_op jit(solution)/shard_map/tae,tbe->ab/dot_general | solution.py:25
  68.3 0.0 all-reduce.2.cloned.1.call-update
  68.3 0.0 copy-done
  68.3 5.2 %fusion.1 = f32[16,160,320]{2,1,0:T(8,128)} fusion(bf16[320,40,1]{0,1,2:T(8,128)(2,1)S(1)} %reshape.21, bf16[16,160,320]{2,1,0:T(8,128)(2,1)} %param.7, bf16[320,40]{0,1:T(8,128)(2,1)S(1)} %copy-done), kind=kOutput, calls=%fused_computation.4 | convolution fusion | flops 131174400 | bytes 4966400 | tf_op jit(solution)/shard_map/tam,mb->tab/dot_general | solution.py:24
  73.5 46.9 %all-gather.4.cloned.1.call-done = bf16[16,320,320]{2,1,0:T(8,128)(2,1)} async-done(((bf16[16,160,320]{2,1,0:T(8,128)(2,1)}), bf16[16,320,320]{2,1,0:T(8,128)(2,1)}) %all-gather.4.cloned.1.call-update) | async-done | bytes 3276816 | tf_op jit(solution)/shard_map/all_gather | solution.py:36
  120.4 93.5 %all-reduce.2.cloned.1.call-done = f32[160,320]{1,0:T(8,128)} async-done(((f32[160,320]{1,0:T(8,128)}), f32[160,320]{1,0:T(8,128)}) %all-reduce.2.cloned.1.call-update) | async-done | bytes 204816 | tf_op jit(solution)/shard_map/psum | solution.py:31
  213.9 7.0 %fusion = bf16[16,160,320]{2,1,0:T(8,128)(2,1)} fusion(f32[16,160,320]{2,1,0:T(8,128)} %fusion.2, f32[16,160,320]{2,1,0:T(8,128)} %fusion.1, bf16[16,320,320]{2,1,0:T(8,128)(2,1)} %all-gather.4.cloned.1.call-done, f32[160,320]{1,0:T(8,128)} %all-reduce.2.cloned.1.call-done), kind=kOutput, calls=%fused_computation.1 | convolution fusion | flops 527667200 | bytes 11673600 | tf_op jit(solution)/shard_map/ac,tcb->tab/dot_general | solution.py:33
  (1 shorter events, 0.0 us)
Async XLA Ops:
  6.5 61.8 %copy-start = (bf16[320,40]{0,1:T(8,128)(2,1)S(1)}, bf16[320,40]{0,1:T(8,128)(2,1)}, u32[]{:S(2)}) copy-start(bf16[320,40]{0,1:T(8,128)(2,1)} %param.10) | copy-start | bytes 76804
  6.5 4.6 %copy-start.3 = (bf16[40,160]{1,0:T(8,128)(2,1)S(1)}, bf16[40,160]{1,0:T(8,128)(2,1)}, u32[]{:S(2)}) copy-start(bf16[40,160]{1,0:T(8,128)(2,1)} %param.11) | copy-start | bytes 38404
  6.5 9.4 %copy-start.2 = (bf16[320,160]{0,1:T(8,128)(2,1)S(1)}, bf16[320,160]{0,1:T(8,128)(2,1)}, u32[]{:S(2)}) copy-start(bf16[320,160]{0,1:T(8,128)(2,1)} %param.9) | copy-start | bytes 307204
  6.5 57.4 %all-gather.6.cloned.1.call-start = ((), (), s32[]{:S(2)}) async-start(), calls=%async_computation.1 | async-start | bytes 5898240 | tf_op jit(solution)/shard_map/all_gather | solution.py:28
  7.3 113.1 %all-gather.4.cloned.1.call-start = ((), (), s32[]{:S(2)}) async-start(), calls=%async_computation | async-start | bytes 5898240 | tf_op jit(solution)/shard_map/all_gather | solution.py:36
  11.1 52.8 %copy-start.1 = (bf16[16,160,320]{2,1,0:T(8,128)(2,1)S(1)}, bf16[16,160,320]{2,1,0:T(8,128)(2,1)}, u32[]{:S(2)}) copy-start(bf16[16,160,320]{2,1,0:T(8,128)(2,1)} %broadcast_select_fusion) | copy-start | bytes 4915204
  11.1 202.8 %all-reduce.2.cloned.1.call-start = ((), (), s32[]{:S(2)}) async-start(), calls=%async_computation.2 | async-start | bytes 491520 | tf_op jit(solution)/shard_map/psum | solution.py:31
Sparse Core Ops, SparseCore 0:
  8.9 54.9 all-gather.5
  65.4 54.8 all-gather.3
  123.8 90.0 all-reduce.1
where the time goes:
time: 228 us; the launch traced here: 227 us
  waiting for transfers between devices  178 us (78%)
  matrix products  21.4 us (9%)
  between operations  13.1 us (6%)
  blocking collectives  11 us (5%)
  other arithmetic  3.77 us (2%)
    psum x1, waiting for transfers between devices, on_device(): density = lax.psum(partial_density, 'occ')  93.5 us
    all_gather x1, waiting for transfers between devices, on_device(): lax.all_gather(masked, 'vir', axis=1, tiled=True)  46.9 us
    all_gather x1, waiting for transfers between devices, on_device(): lax.all_gather(amplitude_triples, 'vir', axis=1, tiled=True)  36.7 us
    dot_general x1, matrix products, on_device(): jnp.einsum('ac,tcb->tab', density, lax.all_gather(masked, 'vir', axis=1,...  6.97 us
    all_gather x1, blocking collectives, on_device(): lax.all_gather(ladder_weight, 'vir', axis=1, tiled=True)  6.43 us
    dot_general x1, matrix products, on_device(): jnp.einsum('tam,mb->tab', cycle_mid, doubles_full, preferred_element_type...  5.16 us
    dot_general x1, matrix products, on_device(): jnp.einsum('tae,eb->tab', masked, ladder_full, preferred_element_type=f32)  4.91 us
    all_gather x1, blocking collectives, on_device(): lax.all_gather(lambda_doubles, 'vir', axis=1, tiled=True)  4.59 us
  transfers between devices with their start and end apart: 3, of which 3 were waited for; matrix products, arithmetic and copies ran while one was open for 8% of the time, Pallas kernels for 0%

commit v1 on v0

--- a/solution.py
+++ b/solution.py
@@ -28,7 +28,7 @@
         lax.all_gather(amplitude_triples, "vir", axis=1, tiled=True),
         preferred_element_type=f32,
     )
-    density = lax.psum(partial_density, "occ")
+    density = jnp.sum(lax.all_gather(partial_density, "occ"), axis=0)
     density = (density / jnp.sqrt(f32(triples_all * width))).astype(jnp.bfloat16)
     density_term = jnp.einsum(
         "ac,tcb->tab",

time: 228 us -> 187 us (0.82)
  waiting for transfers between devices: 178 us -> 137 us
    psum x1 -> x0, waiting for transfers between devices: 93.5 us -> none  [on_device(): density = lax.psum(partial_density, 'occ')]
    all_gather x0 -> x1, waiting for transfers between devices: none -> 30.1 us  [on_device(): density = jnp.sum(lax.all_gather(partial_density, 'occ'), axis=0)]
    all_gather x1, waiting for transfers between devices: 36.7 us -> 54 us  [on_device(): lax.all_gather(amplitude_triples, 'vir', axis=1, tiled=True)]
    all_gather x1, waiting for transfers between devices: 46.9 us -> 51.5 us  [on_device(): lax.all_gather(masked, 'vir', axis=1, tiled=True)]
    reduce_sum x0 -> x1, other arithmetic: none -> 2.35 us  [on_device(): density = jnp.sum(lax.all_gather(partial_density, 'occ'), axis=0)]
  transfers between devices with their start and end apart: 3 -> 3, of which waited for: 3 -> 3; matrix products, arithmetic and copies ran while one was open for 8% -> 7% of each run, Pallas kernels for 0% -> 0%
where the time goes in v1:
time: 187 us; the launch traced here: 185 us
  waiting for transfers between devices  137 us (73%)
  matrix products  19.8 us (11%)
  between operations  13.2 us (7%)
  blocking collectives  10.1 us (5%)
  other arithmetic  4.85 us (3%)
    all_gather x1, waiting for transfers between devices, on_device(): lax.all_gather(amplitude_triples, 'vir', axis=1, tiled=True)  54 us
    all_gather x1, waiting for transfers between devices, on_device(): lax.all_gather(masked, 'vir', axis=1, tiled=True)  51.5 us
    all_gather x1, waiting for transfers between devices, on_device(): density = jnp.sum(lax.all_gather(partial_density, 'occ'), axis=0)  30.1 us
    dot_general x1, matrix products, on_device(): jnp.einsum('ac,tcb->tab', density, lax.all_gather(masked, 'vir', axis=1,...  6.9 us
    all_gather x1, blocking collectives, on_device(): lax.all_gather(ladder_weight, 'vir', axis=1, tiled=True)  5.56 us
    dot_general x1, matrix products, on_device(): jnp.einsum('tam,mb->tab', cycle_mid, doubles_full, preferred_element_type...  5.13 us
    all_gather x1, blocking collectives, on_device(): lax.all_gather(lambda_doubles, 'vir', axis=1, tiled=True)  4.59 us
    dot_general x1, matrix products, on_device(): jnp.einsum('tae,tbe->ab', masked, lax.all_gather(amplitude_triples, 'vir'...  4.43 us
  transfers between devices with their start and end apart: 3, of which 3 were waited for; matrix products, arithmetic and copies ran while one was open for 7% of the time, Pallas kernels for 0%

profile of v1, /device:TPU:8, one launch (start us, length us, event | category | flops | bytes accessed | tf_op | source)
XLA Modules:
  0.0 185.2 jit_solution(13088541682213249340)
XLA Ops:
  6.5 0.0 copy-start
  6.5 0.0 all-gather.8.cloned.1.call-start
  6.5 0.7 all-gather.8.cloned.1.call-update
  7.3 0.0 all-gather.10.cloned.1.call-start
  7.3 0.7 iota_compare_fusion
  8.0 1.8 broadcast_select_fusion
  9.8 0.0 copy-start.1
  9.8 0.0 copy-start.4
  9.8 0.0 copy-start.3
  9.8 54.0 %all-gather.8.cloned.1.call-done = bf16[16,320,320]{2,1,0:T(8,128)(2,1)} async-done(((bf16[16,160,320]{2,1,0:T(8,128)(2,1)}), bf16[16,320,320]{2,1,0:T(8,128)(2,1)}) %all-gather.8.cloned.1.call-update) | async-done | bytes 3276816 | tf_op jit(solution)/shard_map/all_gather | solution.py:28
  63.9 4.4 %convolution_bitcast_fusion = f32[160,320]{1,0:T(8,128)} fusion(bf16[16,160,320]{2,1,0:T(8,128)(2,1)S(1)} %broadcast_select_fusion, bf16[16,320,320]{2,1,0:T(8,128)(2,1)} %all-gather.8.cloned.1.call-done), kind=kOutput, calls=%fused_computation.5 | convolution fusion | flops 524288000 | bytes 5120000 | tf_op jit(solution)/shard_map/tae,tbe->ab/dot_general | solution.py:25
  68.3 0.0 all-gather.10.cloned.1.call-update
  68.3 0.0 all-gather.6.cloned.1.call-start
  68.4 0.0 copy-done.1
  68.4 0.7 all-gather.6.cloned.1.call-update
  69.1 0.0 copy-start.2
  69.1 0.0 copy-done.4
  69.1 4.6 %all-gather.1 = bf16[2,160,40]{1,2,0:T(8,128)(2,1)S(1)} all-gather(bf16[1,160,40]{1,2,0:T(8,128)(2,1)S(1)} %bitcast.29), channel_id=1, replica_groups=mesh['occ'=16,'vir'=2] {'vir'}, dimensions={0}, use_global_device_ids=true | all-gather | bytes 38400 | tf_op jit(solution)/shard_map/all_gather | solution.py:18
  73.7 0.1 reshape.22
  73.8 0.0 copy-done.3
  73.8 5.6 %all_gather.18 = bf16[320,320]{0,1:T(8,128)(2,1)S(1)} all-gather(bf16[320,160]{0,1:T(8,128)(2,1)S(1)} %copy-done.3), channel_id=1, replica_groups=mesh['occ'=16,'vir'=2] {'vir'}, dimensions={1}, use_global_device_ids=true | all-gather | bytes 307200 | tf_op jit(solution)/shard_map/all_gather | solution.py:17
  79.4 0.0 copy-done
  79.4 5.1 %fusion.1 = f32[16,160,320]{2,1,0:T(8,128)} fusion(bf16[320,40,1]{0,1,2:T(8,128)(2,1)S(1)} %reshape.22, bf16[16,160,320]{2,1,0:T(8,128)(2,1)} %param.7, bf16[320,40]{0,1:T(8,128)(2,1)S(1)} %copy-done), kind=kOutput, calls=%fused_computation.4 | convolution fusion | flops 131174400 | bytes 4966400 | tf_op jit(solution)/shard_map/tam,mb->tab/dot_general | solution.py:24
  84.5 0.0 copy-done.2
  84.5 3.3 %fusion.2 = f32[16,160,320]{2,1,0:T(8,128)} fusion(bf16[16,160,320]{2,1,0:T(8,128)(2,1)S(1)} %copy-done.2, bf16[320,320]{0,1:T(8,128)(2,1)S(1)} %all_gather.18), kind=kOutput, calls=%fused_computation.6 | convolution fusion | flops 524288000 | bytes 5120000 | tf_op jit(solution)/shard_map/tae,eb->tab/dot_general | solution.py:20
  87.8 30.1 %all-gather.10.cloned.1.call-done = f32[2560,320]{1,0:T(8,128)} async-done(((f32[160,320]{1,0:T(8,128)}), f32[2560,320]{1,0:T(8,128)}) %all-gather.10.cloned.1.call-update) | async-done | bytes 3276816 | tf_op jit(solution)/shard_map/all_gather | solution.py:31
  117.9 2.4 %reduce_sum.9 = f32[160,320]{1,0:T(8,128)S(1)} reduce(f32[16,160,320]{2,1,0:T(8,128)} %bitcast.28, f32[]{:T(128)} %constant.3.clone.1), dimensions={0}, to_apply=%region_0.1 | reduce | flops 768000 | bytes 3481604 | tf_op jit(solution)/shard_map/reduce_sum | solution.py:31
  120.3 51.5 %all-gather.6.cloned.1.call-done = bf16[16,320,320]{2,1,0:T(8,128)(2,1)} async-done(((bf16[16,160,320]{2,1,0:T(8,128)(2,1)}), bf16[16,320,320]{2,1,0:T(8,128)(2,1)}) %all-gather.6.cloned.1.call-update) | async-done | bytes 3276816 | tf_op jit(solution)/shard_map/all_gather | solution.py:36
  171.8 6.9 %fusion = bf16[16,160,320]{2,1,0:T(8,128)(2,1)} fusion(f32[16,160,320]{2,1,0:T(8,128)} %fusion.2, f32[16,160,320]{2,1,0:T(8,128)} %fusion.1, bf16[16,320,320]{2,1,0:T(8,128)(2,1)} %all-gather.6.cloned.1.call-done, f32[160,320]{1,0:T(8,128)S(1)} %reduce_sum.9), kind=kOutput, calls=%fused_computation.1 | convolution fusion | flops 527667200 | bytes 11673600 | tf_op jit(solution)/shard_map/ac,tcb->tab/dot_general | solution.py:33
  (1 shorter events, 0.0 us)
Async XLA Ops:
  6.5 72.9 %copy-start = (bf16[320,40]{0,1:T(8,128)(2,1)S(1)}, bf16[320,40]{0,1:T(8,128)(2,1)}, u32[]{:S(2)}) copy-start(bf16[320,40]{0,1:T(8,128)(2,1)} %param.10) | copy-start | bytes 76804
  6.5 57.4 %all-gather.8.cloned.1.call-start = ((), (), s32[]{:S(2)}) async-start(), calls=%async_computation.1 | async-start | bytes 5898240 | tf_op jit(solution)/shard_map/all_gather | solution.py:28
  7.3 110.7 %all-gather.10.cloned.1.call-start = ((), (), s32[]{:S(2)}) async-start(), calls=%async_computation.2 | async-start | bytes 4177920 | tf_op jit(solution)/shard_map/all_gather | solution.py:31
  9.8 58.6 %copy-start.1 = (bf16[16,160,320]{2,1,0:T(8,128)(2,1)}, bf16[16,160,320]{2,1,0:T(8,128)(2,1)S(1)}, u32[]{:S(2)}) copy-start(bf16[16,160,320]{2,1,0:T(8,128)(2,1)S(1)} %broadcast_select_fusion) | copy-start | bytes 4915204
  9.8 59.3 %copy-start.4 = (bf16[40,160]{1,0:T(8,128)(2,1)S(1)}, bf16[40,160]{1,0:T(8,128)(2,1)}, u32[]{:S(2)}) copy-start(bf16[40,160]{1,0:T(8,128)(2,1)} %param.11) | copy-start | bytes 38404
  9.8 64.0 %copy-start.3 = (bf16[320,160]{0,1:T(8,128)(2,1)S(1)}, bf16[320,160]{0,1:T(8,128)(2,1)}, u32[]{:S(2)}) copy-start(bf16[320,160]{0,1:T(8,128)(2,1)} %param.9) | copy-start | bytes 307204
  68.3 103.4 %all-gather.6.cloned.1.call-start = ((), (), s32[]{:S(2)}) async-start(), calls=%async_computation | async-start | bytes 5898240 | tf_op jit(solution)/shard_map/all_gather | solution.py:36
  69.1 15.4 %copy-start.2 = (bf16[16,160,320]{2,1,0:T(8,128)(2,1)S(1)}, bf16[16,160,320]{2,1,0:T(8,128)(2,1)}, u32[]{:S(2)}) copy-start(bf16[16,160,320]{2,1,0:T(8,128)(2,1)} %copy-done.1) | copy-start | bytes 4915204
Sparse Core Ops, SparseCore 0:
  8.9 54.9 all-gather.7
  68.5 49.4 all-gather.9
  119.5 52.2 all-gather.5
